TPU v7x, 128 devices: a whole 4x4x4 slice. The times are simulated.
128 devices in a mesh: row: 8 (over x_lo, z), col: 16 (over y, x_hi, core).
Axes of the slice: x: 4 (x_hi: 2, x_lo: 2; x = x_hi * 2 + x_lo), y: 4, z: 4, core: 2. Of those that a mesh axis runs over, the one named last changes fastest.
Arguments:
- amplitudes: bfloat16 [32, 32, 12, 4096], P('row', 'col'), may hold values from -6 to 6
- integrals: bfloat16 [32, 32, 47, 4096], P('row', 'col'), may hold values from -0.125 to 0.125
- pair_lists: int32 [8, 12, 2], replicated, may hold values from 0 to 46, as said below
- tile_counts: int32 [8], replicated, may hold values from 1 to 12, as said below
Outputs:
- symmetric: float32 [32, 32, 12, 4096], P('row', 'col')
Inputs may be any that keep to these rules, and one draw needn't show every extreme that they name: `pair_lists`: each grid row lists 12 distinct ordered pairs of different tiles. `tile_counts`: the largest count equals 12.
All inputs are finite; a program needn't handle non-finite values.
Results may differ from a plain program's by a relative error of at most 0.0029.
Values may be sent and summed in bfloat16 or wider, within the bound.
A program may use at most 128 MiB of HBM per device.

v0:
```python
import jax
import jax.numpy as jnp
from jax import lax
from jax.sharding import PartitionSpec as P

TILE = 64


def spread(block, axis, owner):
    block = jnp.where(lax.axis_index(axis) == owner, block, jnp.zeros_like(block))
    return lax.psum(block, axis)


def on_device(amplitudes, integrals, pair_lists, tile_counts):
    occ_row, occ_col, slot_count, square = amplitudes.shape
    tile_width = TILE
    row_devices = lax.axis_size("row")
    col_devices = lax.axis_size("col")
    col_ratio = col_devices // row_devices
    my_row = lax.axis_index("row")
    my_col = lax.axis_index("col")
    partner_row = my_col // col_ratio
    tile_first = pair_lists[:, :, 0]
    tile_second = pair_lists[:, :, 1]
    packed = jnp.take(integrals, tile_second.reshape(-1), axis=2)
    packed = packed.reshape(occ_row, occ_col, row_devices, slot_count, square)
    received = lax.all_to_all(packed, "row", split_axis=2, concat_axis=0, tiled=True)
    received = received.reshape(occ_row * row_devices, occ_col, slot_count, square)
    piece = lax.all_gather(amplitudes, "col", axis=1, tiled=True)
    piece_count = piece.shape[1]
    left_tiles = piece.reshape(occ_row, piece_count, slot_count, tile_width, tile_width)
    right_tiles = received.reshape(piece_count, occ_col, slot_count, tile_width, tile_width)
    cycle_sum = jnp.einsum(
        "iksac,kjscb->ijsab", left_tiles, right_tiles, preferred_element_type=jnp.float32
    )
    my_count = lax.dynamic_index_in_dim(tile_counts, my_row, 0, keepdims=False)
    live_slots = (jnp.arange(slot_count, dtype=jnp.int32) < my_count).astype(jnp.float32)
    cycle_value = (cycle_sum * live_slots[None, None, :, None, None]).astype(jnp.bfloat16)
    cycle = cycle_value.reshape(occ_row, occ_col, slot_count, square)
    residual_strip = lax.all_gather(cycle, "col", axis=1, tiled=True)
    mirror_part = lax.dynamic_slice_in_dim(residual_strip, my_col % col_ratio * occ_col, occ_col, 0)
    mirror_whole = spread(mirror_part, "row", partner_row)
    mirror_block = lax.dynamic_slice_in_dim(mirror_whole, my_row * occ_row, occ_row, 1)
    mirror_block = mirror_block.reshape(occ_col, occ_row, slot_count, tile_width, tile_width)
    mine_first = lax.dynamic_index_in_dim(tile_first, my_row, 0, keepdims=False)
    mine_second = lax.dynamic_index_in_dim(tile_second, my_row, 0, keepdims=False)
    their_first = lax.dynamic_index_in_dim(tile_first, partner_row, 0, keepdims=False)
    their_second = lax.dynamic_index_in_dim(tile_second, partner_row, 0, keepdims=False)
    pair_match = (
        (mine_first[:, None] == their_second[None, :])
        & (mine_second[:, None] == their_first[None, :])
    ).astype(jnp.bfloat16)
    crossed = jnp.einsum(
        "st,jitba->ijsab", pair_match, mirror_block, preferred_element_type=jnp.float32
    )
    own_part = cycle_value.astype(jnp.float32)
    symmetric = (own_part + crossed) * live_slots[None, None, :, None, None]
    return symmetric.reshape(occ_row, occ_col, slot_count, square)


def solution(mesh):
    return jax.shard_map(
        on_device,
        mesh=mesh,
        in_specs=(P("row", "col", None, None), P("row", "col", None, None), P(), P()),
        out_specs=P("row", "col", None, None),
        check_vma=False,
    )
```

profile of v0, /device:TPU:1, one launch (start us, length us, event | category | flops | bytes accessed | tf_op | source)
XLA Modules:
  0.0 507.0 jit_solution(17754718859662884650)
XLA Ops:
  6.5 2.8 copy.18
  9.3 0.8 fusion.29
  10.2 15.2 %gather_fusion = bf16[96,4,2,4096]{3,2,1,0:T(2,128)(2,1)} fusion(bf16[4,2,47,4096]{3,1,2,0:T(2,128)(2,1)S(1)} %copy-done, s32[1024]{0:T(1024)S(1)} %pad_clamp_fusion), kind=kCustom, calls=%fused_computation | custom fusion | bytes 12583296 | tf_op jit(solution)/shard_map/jit(_take)/gather | solution.py:25
  25.5 8.5 %broadcast_select_fusion.1 = bf16[4,2,8,12,4096]{4,1,3,0,2:T(2,128)(2,1)} fusion(pred[8,12]{1,0:T(8,128)(4,1)S(1)} %compare_and_fusion, bf16[4,2,8,12,4096]{4,1,0,3,2:T(2,128)(2,1)} %bitcast.67), kind=kLoop, calls=%fused_computation.5 | loop fusion | flops 3145728 | bytes 12583008 | tf_op jit(solution)/shard_map/jit(_take)/select_n | solution.py:25
  33.9 6.9 %all-to-all-start = ((bf16[4,2,8,12,4096]{4,1,3,0,2:T(2,128)(2,1)}), bf16[4,2,8,12,4096]{4,1,3,0,2:T(2,128)(2,1)}, u32[]{:S(2)}, u32[]{:S(2)}) async-start(bf16[4,2,8,12,4096]{4,1,3,0,2:T(2,128)(2,1)} %broadcast_select_fusion.1), calls=%async_computation | async-start | bytes 12582912 | tf_op jit(solution)/shard_map/all_to_all | solution.py:27
  41.1 0.6 dynamic_slice.23
  41.7 0.6 compare_convert_fusion
  42.3 101.4 %all-to-all-done = bf16[4,2,8,12,4096]{4,1,3,0,2:T(2,128)(2,1)} async-done(((bf16[4,2,8,12,4096]{4,1,3,0,2:T(2,128)(2,1)}), bf16[4,2,8,12,4096]{4,1,3,0,2:T(2,128)(2,1)}, u32[]{:S(2)}, u32[]{:S(2)}) %all-to-all-start) | async-done | bytes 6291488 | tf_op jit(solution)/shard_map/all_to_all | solution.py:27
  143.6 20.6 %reshape_reshape.3 = bf16[32,2,12,64,64]{4,3,1,2,0:T(8,128)(2,1)} reshape(bf16[8,4,2,1,12,4096]{5,2,4,1,0,3:T(2,128)(2,1)} %bitcast.5) | data formatting | bytes 12582912 | tf_op jit(solution)/shard_map/reshape;reshape | solution.py:32
  164.2 14.4 %copy.19 = bf16[4,32,12,4096]{3,1,0,2:T(8,128)(2,1)} copy(bf16[4,32,12,4096]{3,0,2,1:T(4,128)(2,1)} %all-gather.3.cloned.1.call-done) | data formatting | bytes 25165824 | tf_op jit(solution)/shard_map/all_gather | solution.py:29
  178.6 34.4 %reshape.81 = bf16[4,32,12,64,64,1]{4,3,1,0,2,5:T(8,128)(2,1)} reshape(bf16[4,32,12,4096]{3,1,0,2:T(8,128)(2,1)} %copy.19) | data formatting | bytes 25165824 | tf_op jit(solution)/shard_map/reshape | solution.py:31
  213.0 19.0 %fusion.11 = bf16[4,2,12,64,64]{3,4,0,1,2:T(8,128)(2,1)S(1)} fusion(f32[12]{0:T(128)S(1)} %compare_convert_fusion, bf16[4,32,12,64,64,1]{4,3,1,0,2,5:T(8,128)(2,1)} %reshape.81, bf16[32,2,12,64,64]{4,3,1,2,0:T(8,128)(2,1)} %reshape_reshape.3), kind=kOutput, calls=%fused_computation.12 | convolution fusion | flops 1611399168 | bytes 19660848 | tf_op jit(solution)/shard_map/iksac,kjscb->ijsab/dot_general | solution.py:33
  232.1 1.8 copy.33
  233.8 3.7 reshape.85
  237.5 0.3 all-reduce.2.cloned.1.call-start
  237.8 93.1 %all-gather.5.cloned.1.call-done = bf16[4,32,12,4096]{3,0,2,1:T(4,128)(2,1)} async-done(((bf16[4,2,12,4096]{3,0,2,1:T(4,128)(2,1)}), bf16[4,32,12,4096]{3,0,2,1:T(4,128)(2,1)}) %all-gather.5.cloned.1.call-update) | async-done | bytes 12582928 | tf_op jit(solution)/shard_map/all_gather | solution.py:40
  330.9 10.8 %broadcast_select_fusion = bf16[2,32,12,4096]{3,0,2,1:T(2,128)(2,1)} fusion(pred[]{:T(512)S(6)} %eq.39, bf16[4,32,12,4096]{3,0,2,1:T(4,128)(2,1)} %all-gather.5.cloned.1.call-done, s32[]{:T(128)S(6)} %select_n.65), kind=kLoop, calls=%fused_computation.4 | loop fusion | flops 3145728 | bytes 12582917 | tf_op jit(solution)/shard_map/jit(_where)/select_n | solution.py:10
  341.7 142.5 %all-reduce.2.cloned.1.call-done = bf16[2,32,12,4096]{3,0,2,1:T(2,128)(2,1)} async-done(((bf16[2,32,12,4096]{3,0,2,1:T(2,128)(2,1)}), bf16[2,32,12,4096]{3,0,2,1:T(2,128)(2,1)}) %all-reduce.2.cloned.1.call-update) | async-done | bytes 6291472 | tf_op jit(solution)/shard_map/psum | solution.py:11
  484.3 2.0 constant_dynamic-slice_fusion.4
  486.3 1.0 reshape.86
  487.3 1.1 fusion.5
  488.4 4.3 fusion.3
  492.7 3.6 copy.26
  496.3 4.2 reshape.71
  (20 shorter events, 0.4 us)
Async XLA Ops:
  6.5 3.7 copy-start
  6.5 157.7 %all-gather.3.cloned.1.call-start = ((), (), s32[]{:S(2)}) async-start(), calls=%async_computation.1 | async-start | bytes 13369344 | tf_op jit(solution)/shard_map/all_gather | solution.py:29
  33.9 7.2 %copy-start.3 = (s32[8]{0:T(128)S(1)}, s32[8]{0:T(128)}, u32[]{:S(2)}) copy-start(s32[8]{0:T(128)} %param.7) | copy-start | bytes 100
  33.9 109.7 %all-to-all-start = ((bf16[4,2,8,12,4096]{4,1,3,0,2:T(2,128)(2,1)}), bf16[4,2,8,12,4096]{4,1,3,0,2:T(2,128)(2,1)}, u32[]{:S(2)}, u32[]{:S(2)}) async-start(bf16[4,2,8,12,4096]{4,1,3,0,2:T(2,128)(2,1)} %broadcast_select_fusion.1), calls=%async_computation | async-start | bytes 12582912 | tf_op jit(solution)/shard_map/all_to_all | solution.py:27
  40.9 290.0 %all-gather.5.cloned.1.call-start = ((), (), s32[]{:S(2)}) async-start(), calls=%async_computation.2 | async-start | bytes 13369344 | tf_op jit(solution)/shard_map/all_gather | solution.py:40
  232.0 109.6 %copy-start.2 = (bf16[4,2,12,64,64]{3,4,0,1,2:T(8,128)(2,1)}, bf16[4,2,12,64,64]{3,4,0,1,2:T(8,128)(2,1)S(1)}, u32[]{:S(2)}) copy-start(bf16[4,2,12,64,64]{3,4,0,1,2:T(8,128)(2,1)S(1)} %fusion.11) | copy-start | bytes 2359300
  237.5 246.7 %all-reduce.2.cloned.1.call-start = ((), (), s32[]{:S(2)}) async-start(), calls=%async_computation.3 | async-start | bytes 12582912 | tf_op jit(solution)/shard_map/psum | solution.py:11
  488.4 12.0 %copy-start.1 = (bf16[4,2,47,4096]{3,1,2,0:T(2,128)(2,1)S(1)}, bf16[4,2,47,4096]{3,1,2,0:T(2,128)(2,1)}, u32[]{:S(2)}) copy-start(bf16[4,2,47,4096]{3,1,2,0:T(2,128)(2,1)} %param.5) | copy-start | bytes 9240580
Sparse Core Ops, SparseCore 0:
  9.8 128.3 all-gather.2
  237.6 93.2 all-gather.4
  341.8 142.4 all-reduce.1
where the time goes:
time: 509 us; the launch traced here: 507 us
  waiting for transfers between devices  337 us (66%)
  local copies, waits for them, and re-layouts  105 us (21%)
  other arithmetic  24.1 us (5%)
  matrix products  20.1 us (4%)
  between operations  13.2 us (3%)
  starting transfers between devices  7.4 us (1%)
    psum x1, waiting for transfers between devices, spread(): return lax.psum(block, axis)  143 us
    all_to_all x1, waiting for transfers between devices, on_device(): lax.all_to_all(packed, 'row', split_axis=2, concat_axis=0, tiled=True)  101 us
    all_gather x1, waiting for transfers between devices, on_device(): residual_strip = lax.all_gather(cycle, 'col', axis=1, tiled=True)  93.1 us
    reshape x1, local copies, waits for them, and re-layouts, on_device(): piece.reshape(occ_row, piece_count, slot_count, tile_width, tile_width)  34.4 us
    another operation x1, local copies, waits for them, and re-layouts, on_device(): received.reshape(piece_count, occ_col, slot_count, tile_width, tile_width)  20.6 us
    dot_general x1, matrix products, on_device(): jnp.einsum('iksac,kjscb->ijsab', left_tiles, right_tiles, preferred_eleme...  19 us
    gather x1, local copies, waits for them, and re-layouts, on_device(): packed = jnp.take(integrals, tile_second.reshape(-1), axis=2)  15.2 us
    all_gather x1, local copies, waits for them, and re-layouts, on_device(): piece = lax.all_gather(amplitudes, 'col', axis=1, tiled=True)  14.4 us
  transfers between devices with their start and end apart: 4, of which 3 were waited for; matrix products, arithmetic and copies ran while one was open for 9% of the time, Pallas kernels for 0%

commit v1 on v0

--- a/solution.py
+++ b/solution.py
@@ -2,13 +2,18 @@
 import jax.numpy as jnp
 from jax import lax
 from jax.sharding import PartitionSpec as P
+from jax.lax import all_gather
 
 TILE = 64
 
 
 def spread(block, axis, owner):
     block = jnp.where(lax.axis_index(axis) == owner, block, jnp.zeros_like(block))
-    return lax.psum(block, axis)
+
+    def meet_indices(shard_axis, arr_in):
+        return jnp.sum(all_gather(arr_in, shard_axis), axis=0)
+
+    return meet_indices(axis, block)
 
 
 def on_device(amplitudes, integrals, pair_lists, tile_counts):

time: 509 us -> 875 us (1.72)
  waiting for transfers between devices: 337 us -> 678 us
  other arithmetic: 24.1 us -> 43.1 us
    all_gather x0 -> x1, waiting for transfers between devices: none -> 483 us  [meet_indices(): return jnp.sum(all_gather(arr_in, shard_axis), axis=0)]
    psum x1 -> x0, waiting for transfers between devices: 143 us -> none  [spread(): return lax.psum(block, axis)]
    reduce_sum x0 -> x1, other arithmetic: none -> 20 us  [meet_indices(): return jnp.sum(all_gather(arr_in, shard_axis), axis=0)]
  transfers between devices with their start and end apart: 4 -> 4, of which waited for: 3 -> 3; matrix products, arithmetic and copies ran while one was open for 9% -> 5% of each run, Pallas kernels for 0% -> 0%
where the time goes in v1:
time: 875 us; the launch traced here: 873 us
  waiting for transfers between devices  678 us (77%)
  local copies, waits for them, and re-layouts  112 us (13%)
  other arithmetic  43.1 us (5%)
  matrix products  20.1 us (2%)
  between operations  13.3 us (2%)
    all_gather x1, waiting for transfers between devices, meet_indices(): return jnp.sum(all_gather(arr_in, shard_axis), axis=0)  483 us
    all_to_all x1, waiting for transfers between devices, on_device(): lax.all_to_all(packed, 'row', split_axis=2, concat_axis=0, tiled=True)  101 us
    all_gather x1, waiting for transfers between devices, on_device(): residual_strip = lax.all_gather(cycle, 'col', axis=1, tiled=True)  93.3 us
    reshape x1, local copies, waits for them, and re-layouts, on_device(): piece.reshape(occ_row, piece_count, slot_count, tile_width, tile_width)  34.4 us
    another operation x1, local copies, waits for them, and re-layouts, on_device(): received.reshape(piece_count, occ_col, slot_count, tile_width, tile_width)  20.6 us
    reduce_sum x1, other arithmetic, meet_indices(): return jnp.sum(all_gather(arr_in, shard_axis), axis=0)  20 us
    dot_general x1, matrix products, on_device(): jnp.einsum('iksac,kjscb->ijsab', left_tiles, right_tiles, preferred_eleme...  19 us
  transfers between devices with their start and end apart: 4, of which 3 were waited for; matrix products, arithmetic and copies ran while one was open for 5% of the time, Pallas kernels for 0%

profile of v1, /device:TPU:1, one launch (start us, length us, event | category | flops | bytes accessed | tf_op | source)
XLA Modules:
  0.0 873.3 jit_solution(3558723820480005308)
XLA Ops:
  6.5 2.8 copy.18
  9.3 0.8 fusion.29
  10.2 15.2 %gather_fusion = bf16[96,4,2,4096]{3,2,1,0:T(2,128)(2,1)} fusion(bf16[4,2,47,4096]{3,1,2,0:T(2,128)(2,1)S(1)} %copy-done, s32[1024]{0:T(1024)S(1)} %pad_clamp_fusion), kind=kCustom, calls=%fused_computation | custom fusion | bytes 12583296 | tf_op jit(solution)/shard_map/jit(_take)/gather | solution.py:30
  25.5 8.5 broadcast_select_fusion.1
  33.9 6.9 all-to-all-start
  41.1 0.6 dynamic_slice.23
  42.3 101.4 %all-to-all-done = bf16[4,2,8,12,4096]{4,1,3,0,2:T(2,128)(2,1)} async-done(((bf16[4,2,8,12,4096]{4,1,3,0,2:T(2,128)(2,1)}), bf16[4,2,8,12,4096]{4,1,3,0,2:T(2,128)(2,1)}, u32[]{:S(2)}, u32[]{:S(2)}) %all-to-all-start) | async-done | bytes 6291488 | tf_op jit(solution)/shard_map/all_to_all | solution.py:32
  143.6 20.6 %reshape_reshape.3 = bf16[32,2,12,64,64]{4,3,1,2,0:T(8,128)(2,1)} reshape(bf16[8,4,2,1,12,4096]{5,2,4,1,0,3:T(2,128)(2,1)} %bitcast.5) | data formatting | bytes 12582912 | tf_op jit(solution)/shard_map/reshape;reshape | solution.py:37
  164.2 14.4 %copy.19 = bf16[4,32,12,4096]{3,1,0,2:T(8,128)(2,1)} copy(bf16[4,32,12,4096]{3,0,2,1:T(4,128)(2,1)} %all-gather.5.cloned.1.call-done) | data formatting | bytes 25165824 | tf_op jit(solution)/shard_map/all_gather | solution.py:34
  178.6 34.4 %reshape.82 = bf16[4,32,12,64,64,1]{4,3,1,0,2,5:T(8,128)(2,1)} reshape(bf16[4,32,12,4096]{3,1,0,2:T(8,128)(2,1)} %copy.19) | data formatting | bytes 25165824 | tf_op jit(solution)/shard_map/reshape | solution.py:36
  213.0 19.0 %fusion.11 = bf16[4,2,12,64,64]{3,4,0,1,2:T(8,128)(2,1)S(1)} fusion(f32[12]{0:T(128)S(1)} %compare_convert_fusion, bf16[4,32,12,64,64,1]{4,3,1,0,2,5:T(8,128)(2,1)} %reshape.82, bf16[32,2,12,64,64]{4,3,1,2,0:T(8,128)(2,1)} %reshape_reshape.3), kind=kOutput, calls=%fused_computation.12 | convolution fusion | flops 1611399168 | bytes 19660848 | tf_op jit(solution)/shard_map/iksac,kjscb->ijsab/dot_general | solution.py:38
  232.1 1.6 copy.33
  233.7 3.7 reshape.86
  237.5 93.3 %all-gather.7.cloned.1.call-done = bf16[4,32,12,4096]{3,0,2,1:T(4,128)(2,1)} async-done(((bf16[4,2,12,4096]{3,0,2,1:T(4,128)(2,1)}), bf16[4,32,12,4096]{3,0,2,1:T(4,128)(2,1)}) %all-gather.7.cloned.1.call-update) | async-done | bytes 12582928 | tf_op jit(solution)/shard_map/all_gather | solution.py:45
  330.8 9.8 %broadcast_select_fusion = bf16[2,32,12,4096]{3,0,2,1:T(2,128)(2,1)S(1)} fusion(pred[]{:T(512)S(6)} %eq.39, bf16[4,32,12,4096]{3,0,2,1:T(4,128)(2,1)} %all-gather.7.cloned.1.call-done, s32[]{:T(128)S(6)} %select_n.65), kind=kLoop, calls=%fused_computation.4 | loop fusion | flops 3145728 | bytes 12582917 | tf_op jit(solution)/shard_map/jit(_where)/select_n | solution.py:11
  340.6 7.1 copy.23
  347.7 482.8 %all-gather.9.cloned.1.call-done = bf16[16,32,12,4096]{3,1,2,0:T(8,128)(2,1)} async-done(((bf16[2,32,12,4096]{3,1,2,0:T(8,128)(2,1)}), bf16[16,32,12,4096]{3,1,2,0:T(8,128)(2,1)}) %all-gather.9.cloned.1.call-update) | async-done | bytes 50331664 | tf_op jit(solution)/shard_map/all_gather | solution.py:14
  830.5 20.0 %reduce_sum.12 = bf16[2,32,12,4096]{3,1,2,0:T(8,128)(2,1)} reduce(bf16[8,2,32,12,4096]{4,2,3,1,0:T(8,128)(2,1)} %bitcast.68, bf16[]{:T(256)} %constant.74.clone.1), dimensions={0}, to_apply=%region_0.1 | reduce | flops 22020096 | bytes 56623104 | tf_op jit(solution)/shard_map/reduce_sum | solution.py:14
  850.5 1.9 constant_dynamic-slice_fusion.4
  852.4 1.3 reshape.70
  853.7 1.1 fusion.5
  854.8 4.3 fusion.3
  859.1 3.6 copy.26
  862.6 4.2 reshape.71
  (22 shorter events, 1.0 us)
Async XLA Ops:
  6.5 3.7 copy-start
  6.5 157.7 %all-gather.5.cloned.1.call-start = ((), (), s32[]{:S(2)}) async-start(), calls=%async_computation.1 | async-start | bytes 13369344 | tf_op jit(solution)/shard_map/all_gather | solution.py:34
  33.9 7.2 copy-start.3
  33.9 109.7 %all-to-all-start = ((bf16[4,2,8,12,4096]{4,1,3,0,2:T(2,128)(2,1)}), bf16[4,2,8,12,4096]{4,1,3,0,2:T(2,128)(2,1)}, u32[]{:S(2)}, u32[]{:S(2)}) async-start(bf16[4,2,8,12,4096]{4,1,3,0,2:T(2,128)(2,1)} %broadcast_select_fusion.1), calls=%async_computation | async-start | bytes 12582912 | tf_op jit(solution)/shard_map/all_to_all | solution.py:32
  40.9 289.9 %all-gather.7.cloned.1.call-start = ((), (), s32[]{:S(2)}) async-start(), calls=%async_computation.2 | async-start | bytes 13369344 | tf_op jit(solution)/shard_map/all_gather | solution.py:45
  232.0 108.5 %copy-start.2 = (bf16[4,2,12,64,64]{3,4,0,1,2:T(8,128)(2,1)}, bf16[4,2,12,64,64]{3,4,0,1,2:T(8,128)(2,1)S(1)}, u32[]{:S(2)}) copy-start(bf16[4,2,12,64,64]{3,4,0,1,2:T(8,128)(2,1)S(1)} %fusion.11) | copy-start | bytes 2359300
  237.4 593.2 %all-gather.9.cloned.1.call-start = ((), (), s32[]{:S(2)}) async-start(), calls=%async_computation.3 | async-start | bytes 56623104 | tf_op jit(solution)/shard_map/all_gather | solution.py:14
  854.8 12.0 %copy-start.1 = (bf16[4,2,47,4096]{3,1,2,0:T(2,128)(2,1)S(1)}, bf16[4,2,47,4096]{3,1,2,0:T(2,128)(2,1)}, u32[]{:S(2)}) copy-start(bf16[4,2,47,4096]{3,1,2,0:T(2,128)(2,1)} %param.5) | copy-start | bytes 9240580
Sparse Core Ops, SparseCore 0:
  9.8 128.3 all-gather.4
  237.5 93.2 all-gather.6
  347.8 482.6 all-gather.8
